TPU v7x, 256 devices: a whole 4x4x8 slice. The times are simulated.
256 devices in a mesh: dp: 8 (over z_lo, x), seq: 32 (over y, z_hi, core).
Axes of the slice: x: 4, y: 4, z: 8 (z_hi: 4, z_lo: 2; z = z_hi * 2 + z_lo), core: 2. Of those that a mesh axis runs over, the one named last changes fastest.
Arguments:
- queries: bfloat16 [8, 4096, 4096], P('dp', 'seq'), may hold values from -5 to 5
- rotated_key_rows: bfloat16 [8, 4096, 512], P('dp', 'seq'), may hold values from -5 to 5
- hidden_states: bfloat16 [8, 4096, 8192], P('dp', 'seq'), may hold values from -6 to 6
- block_order: int32 [64], replicated, may hold values from 0 to 63, each once
- first_weight: bfloat16 [8192, 512], replicated, may hold values from -0.0625 to 0.0625
- first_bias: float32 [512], replicated, may hold values from -3 to 3
- output_weight: bfloat16 [4, 512], replicated, may hold values from -0.25 to 0.25
- output_bias: float32 [4], replicated, may hold values from -1 to 1
Outputs:
- token_attention_mass: float32 [8, 4, 4096], P('dp', None, 'seq')
- loss_value: float32 [], replicated
- step_first: float32 [8192, 512], P('seq')
- output_weight_step: float32 [4, 512], replicated
- step_bias: float32 [512], replicated
- grad_bias: float32 [4], replicated
All inputs are finite; a program needn't handle non-finite values.
Results may differ from a plain program's by a relative error of at most 0.0023.
Values may be sent and summed in bfloat16 or wider, within the bound.
A program may use at most 64 MiB of HBM per device.

v0:
```python
import math
import jax
import jax.numpy as jnp
from jax import lax
from jax.sharding import PartitionSpec as P

D = 8192
KEY_VALUE_HEADS = 4
HEAD_SIZE = 128
RETAIN_HIDDEN = 512
BLK = 64
QUERY_GROUP_SIZE = 8


def key_places(block_order, offset, amount):
    row_ids = offset + lax.iota(jnp.int32, amount)
    block_ids = row_ids // BLK
    block_table = lax.iota(jnp.int32, block_order.shape[0])
    anchor = jnp.sum(
        jnp.where(block_ids[:, None] == block_table[None, :], block_order[None, :], 0), axis=1
    )
    return anchor * BLK + row_ids % BLK


def raw_scores(head_queries, mass_portion):
    head_keys = mass_portion.reshape(mass_portion.shape[0], KEY_VALUE_HEADS, HEAD_SIZE)
    return jnp.einsum(
        "tkgd,nkd->kgtn", head_queries, head_keys, preferred_element_type=jnp.float32
    ) * HEAD_SIZE ** (-0.5)


def blockwise(mass_portion, offset, update, carried):
    rows_here = mass_portion.shape[0]
    inner = math.gcd(rows_here, BLK)

    def visit_block(step_index, running):
        local_start = step_index * inner
        sub_rows = lax.dynamic_slice_in_dim(mass_portion, local_start, inner, 0)
        return update(running, sub_rows, offset + local_start)

    return lax.fori_loop(0, rows_here // inner, visit_block, carried)


def normalizer_step(running, mass_portion, key_start, head_queries, query_pos, block_order):
    highest, summed = running
    key_pos = key_places(block_order, key_start, mass_portion.shape[0])

    def normalizer_compute_step():
        scores = raw_scores(head_queries, mass_portion)
        visible = query_pos[:, None] >= key_pos[None, :]
        masked = jnp.where(visible, scores, -1e30)
        raised = jnp.maximum(highest, jnp.max(masked, axis=-1))
        exponents = jnp.where(visible, jnp.exp(masked - raised[..., None]), 0.0)
        return (raised, summed * jnp.exp(highest - raised) + jnp.sum(exponents, axis=-1))

    return lax.cond(
        jnp.min(key_pos) > jnp.max(query_pos), lambda: (highest, summed), normalizer_compute_step
    )


def mass_step(mass_portion, key_start, head_queries, query_pos, log_total, block_order):
    amount = mass_portion.shape[0]
    key_pos = key_places(block_order, key_start, amount)

    def mass_compute_step():
        scores = raw_scores(head_queries, mass_portion)
        visible = query_pos[:, None] >= key_pos[None, :]
        masked = jnp.where(visible, scores, -1e30)
        weights = jnp.where(visible, jnp.exp(masked - log_total[..., None]), 0.0)
        return jnp.sum(weights, axis=(1, 2)) / QUERY_GROUP_SIZE

    return lax.cond(
        jnp.min(key_pos) > jnp.max(query_pos),
        lambda: jnp.zeros((KEY_VALUE_HEADS, amount), jnp.float32),
        mass_compute_step,
    )


def normalized_scores(value_rows, square_sum, entries):
    return value_rows / jnp.sqrt(square_sum / entries + 1e-06)


def per_device(
    queries,
    rotated_key_rows,
    hidden_states,
    block_order,
    first_weight,
    first_bias,
    output_weight,
    output_bias,
):
    local_row_slice = queries.shape[1]
    total_length = local_row_slice * lax.axis_size("seq")
    head_queries = queries.reshape(local_row_slice, KEY_VALUE_HEADS, QUERY_GROUP_SIZE, HEAD_SIZE)
    local_key_rows = rotated_key_rows.reshape(local_row_slice, KEY_VALUE_HEADS * HEAD_SIZE)
    query_pos = key_places(block_order, lax.axis_index("seq") * local_row_slice, local_row_slice)
    start_state = (
        jnp.full((KEY_VALUE_HEADS, QUERY_GROUP_SIZE, local_row_slice), -1e30, jnp.float32),
        jnp.zeros((KEY_VALUE_HEADS, QUERY_GROUP_SIZE, local_row_slice), jnp.float32),
    )

    def norm_update(running, sub_rows, key_start):
        return normalizer_step(running, sub_rows, key_start, head_queries, query_pos, block_order)

    empty_mass = jnp.zeros((KEY_VALUE_HEADS, total_length), jnp.float32)
    keys_whole = lax.all_gather(local_key_rows, "seq", axis=0, tiled=True)
    highest, summed = blockwise(keys_whole, 0, norm_update, start_state)
    log_total = highest + jnp.log(summed)

    def add_kept(collected, sub_rows, key_start):
        term = mass_step(sub_rows, key_start, head_queries, query_pos, log_total, block_order)
        return lax.dynamic_update_slice_in_dim(collected, term, key_start, 1)

    column_mass = blockwise(keys_whole, 0, add_kept, empty_mass)
    key_attention_mass = lax.psum_scatter(column_mass, "seq", scatter_dimension=1, tiled=True)
    tokens_in = hidden_states.reshape(local_row_slice, hidden_states.shape[2])
    pre_act = jnp.dot(tokens_in, first_weight, preferred_element_type=jnp.float32) + first_bias
    hidden = jax.nn.silu(pre_act).astype(jnp.bfloat16)
    predicted_scores = (
        lax.dot_general(
            output_weight, hidden, (((1,), (1,)), ((), ())), preferred_element_type=jnp.float32
        )
        + output_bias[:, None]
    )
    score_residue = predicted_scores - jnp.log(1.0 + key_attention_mass)
    loss_part = 0.5 * jnp.sum(score_residue * score_residue) / total_length
    out_grad = score_residue / total_length
    bias_part = jnp.sum(out_grad, axis=1)
    second_part = jnp.dot(out_grad, hidden.astype(jnp.float32), precision=lax.Precision.HIGHEST)
    back_grad = jnp.dot(
        out_grad.T, output_weight.astype(jnp.float32), precision=lax.Precision.HIGHEST
    )
    gate_value = jax.nn.sigmoid(pre_act)
    slope_grad = back_grad * gate_value * (1.0 + pre_act * (1.0 - gate_value))
    first_bias_part = jnp.sum(slope_grad, axis=0)
    slope_half = slope_grad.astype(jnp.bfloat16)
    columns_all = lax.all_to_all(tokens_in, "seq", split_axis=1, concat_axis=0, tiled=True)
    slope_all = lax.all_gather(slope_half, "seq", axis=0, tiled=True)
    first_shard = lax.dot_general(
        columns_all, slope_all, (((0,), (0,)), ((), ())), preferred_element_type=jnp.float32
    )
    output_total, first_bias_total, bias_total, loss_total = lax.psum(
        (second_part, first_bias_part, bias_part, loss_part), ("dp", "seq")
    )
    first_grad = lax.psum(first_shard, "dp")
    first_square = lax.psum(jnp.sum(first_grad * first_grad), "seq")
    step_first = normalized_scores(first_grad, first_square, D * RETAIN_HIDDEN)
    output_weight_step = normalized_scores(
        output_total, jnp.sum(output_total * output_total), RETAIN_HIDDEN * KEY_VALUE_HEADS
    )
    step_bias = normalized_scores(
        first_bias_total, jnp.sum(first_bias_total * first_bias_total), RETAIN_HIDDEN
    )
    return (
        key_attention_mass.reshape(1, KEY_VALUE_HEADS, local_row_slice),
        loss_total,
        step_first,
        output_weight_step,
        step_bias,
        bias_total,
    )


def solution(mesh):
    in_specs = (
        P("dp", "seq", None),
        P("dp", "seq", None),
        P("dp", "seq", None),
        P(),
        P(),
        P(),
        P(),
        P(),
    )
    out_specs = (P("dp", None, "seq"), P(), P("seq", None), P(), P(), P())
    return jax.shard_map(
        per_device, mesh=mesh, in_specs=in_specs, out_specs=out_specs, check_vma=False
    )
```

profile of v0, /device:TPU:1, one launch (start us, length us, event | category | flops | bytes accessed | tf_op | source)
XLA Modules:
  0.0 925.9 jit_solution(2229353486682803280)
XLA Ops:
  8.0 1.6 copy.39
  11.0 64.1 %all-gather.6.cloned.1.call-done = bf16[1,4096,512]{2,1,0:T(8,128)(2,1)} async-done(((bf16[1,128,512]{2,1,0:T(8,128)(2,1)}), bf16[1,4096,512]{2,1,0:T(8,128)(2,1)}) %all-gather.6.cloned.1.call-update) | async-done | bytes 4194320 | tf_op jit(solution)/shard_map/all_gather | solution.py:107
  75.1 206.3 %while.32 = (s32[]{:T(128)}, f32[4,8,128]{2,1,0:T(8,128)S(1)}, f32[4,8,128]{2,1,0:T(8,128)S(1)}, s32[64]{0:T(128)S(1)}, s32[]{:T(128)}, /*index=5*/s32[128]{0:T(...) while((s32[]{:T(128)}, f32[4,8,128]{2,1,0:T(8,128)S(1)}, ...), condition=%wide.region_9.10_spmd, body=%wide.region_2.9_spmd.sunk | while | flops 68712320 | bytes 3713545 | solution.py:41
  79.5 1.7 conditional.4
  83.4 1.7 conditional.4
  87.3 1.7 conditional.4
  91.3 1.7 conditional.4
  108.4 1.7 conditional.4
  112.3 1.7 conditional.4
  118.5 1.7 conditional.4
  122.4 1.7 conditional.4
  128.5 1.7 conditional.4
  132.4 1.7 conditional.4
  138.6 1.7 conditional.4
  144.7 1.7 conditional.4
  153.0 1.7 conditional.4
  156.9 1.7 conditional.4
  160.9 1.7 conditional.4
  169.2 1.7 conditional.4
  173.1 1.7 conditional.4
  177.0 1.7 conditional.4
  181.0 1.7 conditional.4
  184.9 1.7 conditional.4
  193.2 1.7 conditional.4
  199.3 1.7 conditional.4
  203.3 1.7 conditional.4
  213.8 1.7 conditional.4
  217.7 1.7 conditional.4
  221.6 1.7 conditional.4
  225.6 1.7 conditional.4
  231.7 1.7 conditional.4
  235.6 1.7 conditional.4
  239.5 1.7 conditional.4
  243.4 1.7 conditional.4
  249.6 1.7 conditional.4
  253.5 1.7 conditional.4
  257.4 1.7 conditional.4
  261.3 1.7 conditional.4
  265.2 1.7 conditional.4
  269.1 1.7 conditional.4
  279.7 1.7 conditional.4
  281.5 212.6 %while.33 = (s32[]{:T(128)}, f32[4,4096]{1,0:T(4,128)S(1)}, s32[64]{0:T(128)S(1)}, s32[]{:T(128)}, s32[128]{0:T(128)S(1)}, /*index=5*/bf16[4096,512]{1,0:T(8,128...) while((s32[]{:T(128)}, f32[4,4096]{1,0:T(4,128)S(1)}, ...), condition=%wide.region_16.17_spmd, body=%wide.region_10.16_spmd.sunk | while | flops 68441992 | bytes 1416701 | solution.py:41
  286.0 1.6 conditional.5
  326.6 1.6 conditional.5
  336.9 1.6 conditional.5
  347.2 1.6 conditional.5
  386.9 1.6 conditional.5
  394.8 1.6 conditional.5
  409.8 1.6 conditional.5
  425.0 1.6 conditional.5
  432.9 1.6 conditional.5
  455.0 1.6 conditional.5
  465.3 1.6 conditional.5
  494.1 2.0 copy.51
  496.2 4.8 multiply_convert_fusion
  501.0 164.5 %reduce-scatter.4.cloned.1.call-done = f32[128,4]{1,0:T(8,128)} async-done(((f32[4096,4]{1,0:T(8,128)}), f32[128,4]{1,0:T(8,128)}) %reduce-scatter.4.cloned.1.call-update) | async-done | bytes 2064
  668.3 2.5 copy.42
  670.8 63.7 %all_to_all.19 = bf16[128,32,256]{0,2,1:T(8,128)(2,1)S(1)} all-to-all(bf16[128,32,256]{0,2,1:T(8,128)(2,1)} %bitcast.50), channel_id=1, replica_groups=mesh['dp'=8,'seq'=32] {'seq'}, dimensions={1} | all-to-all | bytes 4194304 | tf_op jit(solution)/shard_map/all_to_all | solution.py:138
  734.5 2.9 copy.43
  737.4 19.9 %all-gather.4.cloned.1.call-done = bf16[4096,512]{1,0:T(8,128)(2,1)} async-done(((bf16[128,512]{1,0:T(8,128)(2,1)}), bf16[4096,512]{1,0:T(8,128)(2,1)}) %all-gather.4.cloned.1.call-update) | async-done | bytes 4194320 | tf_op jit(solution)/shard_map/all_gather | solution.py:139
  757.3 4.9 convolution_bitcast_fusion
  763.1 77.0 %all-reduce = (f32[]{:T(128)}, f32[4,512]{1,0:T(4,128)S(1)}, f32[512]{0:T(512)S(1)}, f32[4]{0:T(128)}) all-reduce(f32[]{:T(128)S(6)} %div.87, f32[4,512]{1,0:T(4,128)S(1)} %fusion.20, f32[512]{0:T(512)S(1)} %get-tuple-element.630, f32[4]{0:T(128)S(1)} %get-tuple-element.583), channel_id=1, replica_groups=mesh['dp'=8,'seq'=32] {'dp','seq'}, use_global_device_ids=true, to_apply=%region_19.20 | all-reduce | flops 2565 | bytes 20520 | tf_op jit(solution)/shard_map/psum | solution.py:143
  843.3 1.8 multiply_reduce_fusion
  845.7 70.9 %psum.44 = f32[]{:T(128)} all-reduce(f32[]{:T(128)} %multiply_reduce_fusion), channel_id=1, replica_groups=mesh['dp'=8,'seq'=32] {'seq'}, use_global_device_ids=true, to_apply=%region_22.23 | all-reduce | flops 1 | bytes 8 | tf_op jit(solution)/shard_map/psum | solution.py:147
  (1138 shorter events, 297.1 us)
Async XLA Ops:
  7.2 659.3 %copy-start = (bf16[4,512]{1,0:T(4,128)(2,1)S(1)}, bf16[4,512]{1,0:T(4,128)(2,1)}, u32[]{:S(2)}) copy-start(bf16[4,512]{1,0:T(4,128)(2,1)} %param.22) | copy-start | bytes 12292
  7.2 3.1 copy-start.4
  7.2 67.9 %all-gather.6.cloned.1.call-start = ((), (), s32[]{:S(2)}) async-start(), calls=%async_computation.4 | async-start | bytes 4325376 | tf_op jit(solution)/shard_map/all_gather | solution.py:107
  7.9 657.6 %reduce-scatter.4.cloned.1.call-start = ((), (), s32[]{:S(2)}) async-start(), calls=%async_computation.5 | async-start | bytes 2162688
  494.1 2.1 copy-start.1
  494.1 2.1 copy-start.2
  496.1 170.4 %copy-start.5 = (f32[4]{0:T(128)S(1)}, f32[4]{0:T(128)}, u32[]{:S(2)}) copy-start(f32[4]{0:T(128)} %param.23) | copy-start | bytes 52
  496.1 261.2 %all-gather.4.cloned.1.call-start = ((), (), s32[]{:S(2)}) async-start(), calls=%async_computation.2 | async-start | bytes 4325376 | tf_op jit(solution)/shard_map/all_gather | solution.py:139
  666.4 68.1 %copy-start.3 = (f32[4,128]{1,0:T(4,128)}, f32[4,128]{1,0:T(4,128)S(1)}, u32[]{:S(2)}) copy-start(f32[4,128]{1,0:T(4,128)S(1)} %copy.52) | copy-start | bytes 6148
  668.2 175.1 %all-reduce.3.cloned.1.call-start = ((), (), s32[]{:S(2)}) async-start(), calls=%async_computation.3 | async-start | bytes 1048576 | tf_op jit(solution)/shard_map/psum | solution.py:146
Sparse Core Ops, SparseCore 0:
  10.6 64.5 all-gather.5
  496.2 169.2 reduce-scatter.3
  668.7 88.6 all-gather.3
  762.4 72.5 all-reduce.2
where the time goes:
time: 935 us; the launch traced here: 926 us
  waiting for transfers between devices  249 us (27%)
  blocking collectives  212 us (23%)
  loops' own time  175 us (19%)
  other arithmetic  128 us (14%)
  local copies, waits for them, and re-layouts  92.1 us (10%)
  matrix products  52.9 us (6%)
  between operations  16.7 us (2%)
    another operation x2, loops' own time, blockwise(): return lax.fori_loop(0, rows_here // inner, visit_block, carried)  171 us
    unnamed x5, waiting for transfers between devices  165 us
    psum x1, blocking collectives, per_device(): lax.psum((second_part, first_bias_part, bias_part, loss_part), ('dp', 'se...  77 us
    psum x1, blocking collectives, per_device(): first_square = lax.psum(jnp.sum(first_grad * first_grad), 'seq')  70.9 us
    dynamic_slice x76, local copies, waits for them, and re-layouts, visit_block(): sub_rows = lax.dynamic_slice_in_dim(mass_portion, local_start, inner, 0)  64.7 us
    all_gather x1, waiting for transfers between devices, per_device(): keys_whole = lax.all_gather(local_key_rows, 'seq', axis=0, tiled=True)  64.1 us
    all_to_all x1, blocking collectives, per_device(): lax.all_to_all(tokens_in, 'seq', split_axis=1, concat_axis=0, tiled=True)  63.7 us
    reduce_min x64, other arithmetic, normalizer_step(): jnp.min(key_pos) > jnp.max(query_pos)  41.8 us
  transfers between devices with their start and end apart: 4, of which 3 were waited for; matrix products, arithmetic and copies ran while one was open for 2% of the time, Pallas kernels for 0%

commit v1 on v0

--- a/solution.py
+++ b/solution.py
@@ -10,6 +10,12 @@
 RETAIN_HIDDEN = 512
 BLK = 64
 QUERY_GROUP_SIZE = 8
+
+
+def recover_outputs(axis_key, raw, mesh_name):
+    for nth in (axis_key, mesh_name):
+        raw = lax.psum(raw, nth)
+    return raw
 
 
 def key_places(block_order, offset, amount):
@@ -140,8 +146,8 @@
     first_shard = lax.dot_general(
         columns_all, slope_all, (((0,), (0,)), ((), ())), preferred_element_type=jnp.float32
     )
-    output_total, first_bias_total, bias_total, loss_total = lax.psum(
-        (second_part, first_bias_part, bias_part, loss_part), ("dp", "seq")
+    output_total, first_bias_total, bias_total, loss_total = recover_outputs(
+        "seq", (second_part, first_bias_part, bias_part, loss_part), "dp"
     )
     first_grad = lax.psum(first_shard, "dp")
     first_square = lax.psum(jnp.sum(first_grad * first_grad), "seq")

time: 935 us -> 1030 us (1.10)
  waiting for transfers between devices: 249 us -> 321 us
  blocking collectives: 212 us -> 227 us
    psum x1, waiting for transfers between devices: 0.01 us -> 71.9 us  [per_device(): first_grad = lax.psum(first_shard, 'dp')]
    psum x2, blocking collectives: 148 us -> 163 us  [recover_outputs(): raw = lax.psum(raw, nth)]
  transfers between devices with their start and end apart: 4 -> 4, of which waited for: 3 -> 4; matrix products, arithmetic and copies ran while one was open for 2% -> 1% of each run, Pallas kernels for 0% -> 0%
where the time goes in v1:
time: 1030 us; the launch traced here: 1010 us
  waiting for transfers between devices  321 us (31%)
  blocking collectives  227 us (22%)
  loops' own time  175 us (17%)
  other arithmetic  128 us (12%)
  local copies, waits for them, and re-layouts  92.1 us (9%)
  matrix products  52.9 us (5%)
  between operations  16.6 us (2%)
    another operation x2, loops' own time, blockwise(): return lax.fori_loop(0, rows_here // inner, visit_block, carried)  171 us
    unnamed x5, waiting for transfers between devices  165 us
    psum x2, blocking collectives, recover_outputs(): raw = lax.psum(raw, nth)  163 us
    psum x1, waiting for transfers between devices, per_device(): first_grad = lax.psum(first_shard, 'dp')  71.9 us
    dynamic_slice x76, local copies, waits for them, and re-layouts, visit_block(): sub_rows = lax.dynamic_slice_in_dim(mass_portion, local_start, inner, 0)  64.7 us
    all_gather x1, waiting for transfers between devices, per_device(): keys_whole = lax.all_gather(local_key_rows, 'seq', axis=0, tiled=True)  64.1 us
    all_to_all x1, blocking collectives, per_device(): lax.all_to_all(tokens_in, 'seq', split_axis=1, concat_axis=0, tiled=True)  63.7 us
    reduce_min x64, other arithmetic, normalizer_step(): jnp.min(key_pos) > jnp.max(query_pos)  41.8 us
  transfers between devices with their start and end apart: 4, of which 4 were waited for; matrix products, arithmetic and copies ran while one was open for 1% of the time, Pallas kernels for 0%

profile of v1, /device:TPU:1, one launch (start us, length us, event | category | flops | bytes accessed | tf_op | source)
XLA Modules:
  0.0 1012.8 jit_solution(16904194593461795754)
XLA Ops:
  8.0 1.6 copy.39
  11.0 64.1 %all-gather.6.cloned.1.call-done = bf16[1,4096,512]{2,1,0:T(8,128)(2,1)} async-done(((bf16[1,128,512]{2,1,0:T(8,128)(2,1)}), bf16[1,4096,512]{2,1,0:T(8,128)(2,1)}) %all-gather.6.cloned.1.call-update) | async-done | bytes 4194320 | tf_op jit(solution)/shard_map/all_gather | solution.py:113
  75.1 206.3 %while.32 = (s32[]{:T(128)}, f32[4,8,128]{2,1,0:T(8,128)S(1)}, f32[4,8,128]{2,1,0:T(8,128)S(1)}, s32[64]{0:T(128)S(1)}, s32[]{:T(128)}, /*index=5*/s32[128]{0:T(...) while((s32[]{:T(128)}, f32[4,8,128]{2,1,0:T(8,128)S(1)}, ...), condition=%wide.region_9.10_spmd, body=%wide.region_2.9_spmd.sunk | while | flops 68712320 | bytes 3713545 | solution.py:47
  79.5 1.7 conditional.4
  83.4 1.7 conditional.4
  87.3 1.7 conditional.4
  91.3 1.7 conditional.4
  108.4 1.7 conditional.4
  112.3 1.7 conditional.4
  118.5 1.7 conditional.4
  122.4 1.7 conditional.4
  128.5 1.7 conditional.4
  132.4 1.7 conditional.4
  138.6 1.7 conditional.4
  144.7 1.7 conditional.4
  153.0 1.7 conditional.4
  156.9 1.7 conditional.4
  160.9 1.7 conditional.4
  169.2 1.7 conditional.4
  173.1 1.7 conditional.4
  177.0 1.7 conditional.4
  181.0 1.7 conditional.4
  184.9 1.7 conditional.4
  193.2 1.7 conditional.4
  199.3 1.7 conditional.4
  203.3 1.7 conditional.4
  213.8 1.7 conditional.4
  217.7 1.7 conditional.4
  221.6 1.7 conditional.4
  225.6 1.7 conditional.4
  231.7 1.7 conditional.4
  235.6 1.7 conditional.4
  239.5 1.7 conditional.4
  243.4 1.7 conditional.4
  249.6 1.7 conditional.4
  253.5 1.7 conditional.4
  257.4 1.7 conditional.4
  261.3 1.7 conditional.4
  265.2 1.7 conditional.4
  269.1 1.7 conditional.4
  279.7 1.7 conditional.4
  281.5 212.6 %while.33 = (s32[]{:T(128)}, f32[4,4096]{1,0:T(4,128)S(1)}, s32[64]{0:T(128)S(1)}, s32[]{:T(128)}, s32[128]{0:T(128)S(1)}, /*index=5*/bf16[4096,512]{1,0:T(8,128...) while((s32[]{:T(128)}, f32[4,4096]{1,0:T(4,128)S(1)}, ...), condition=%wide.region_16.17_spmd, body=%wide.region_10.16_spmd.sunk | while | flops 68441992 | bytes 1416701 | solution.py:47
  286.0 1.6 conditional.5
  326.6 1.6 conditional.5
  336.9 1.6 conditional.5
  347.2 1.6 conditional.5
  386.9 1.6 conditional.5
  394.8 1.6 conditional.5
  425.0 1.6 conditional.5
  432.9 1.6 conditional.5
  455.0 1.6 conditional.5
  465.3 1.6 conditional.5
  494.1 2.0 copy.51
  496.2 4.8 multiply_convert_fusion
  501.0 164.5 %reduce-scatter.4.cloned.1.call-done = f32[128,4]{1,0:T(8,128)} async-done(((f32[4096,4]{1,0:T(8,128)}), f32[128,4]{1,0:T(8,128)}) %reduce-scatter.4.cloned.1.call-update) | async-done | bytes 2064
  668.3 2.5 copy.42
  670.8 63.7 %all_to_all.19 = bf16[128,32,256]{0,2,1:T(8,128)(2,1)S(1)} all-to-all(bf16[128,32,256]{0,2,1:T(8,128)(2,1)} %bitcast.50), channel_id=1, replica_groups=mesh['dp'=8,'seq'=32] {'seq'}, dimensions={1} | all-to-all | bytes 4194304 | tf_op jit(solution)/shard_map/all_to_all | solution.py:144
  734.5 2.9 copy.43
  737.4 19.9 %all-gather.4.cloned.1.call-done = bf16[4096,512]{1,0:T(8,128)(2,1)} async-done(((bf16[128,512]{1,0:T(8,128)(2,1)}), bf16[4096,512]{1,0:T(8,128)(2,1)}) %all-gather.4.cloned.1.call-update) | async-done | bytes 4194320 | tf_op jit(solution)/shard_map/all_gather | solution.py:145
  757.3 4.9 convolution_bitcast_fusion
  763.1 71.9 %all-reduce.4.cloned.1.call-done = f32[256,512]{0,1:T(8,128)} async-done(((f32[256,512]{0,1:T(8,128)}), f32[256,512]{0,1:T(8,128)}) %all-reduce.4.cloned.1.call-update) | async-done | bytes 524304 | tf_op jit(solution)/shard_map/psum | solution.py:152
  835.0 1.8 multiply_reduce_fusion
  836.8 137.7 %all-reduce = (f32[]{:T(128)}, f32[]{:T(128)}, f32[4,512]{1,0:T(4,128)S(1)}, f32[512]{0:T(512)S(1)}, f32[4]{0:T(128)S(1)}) all-reduce(f32[]{:T(128)S(6)} %div.87, f32[]{:T(128)} %multiply_reduce_fusion, f32[4,512]{1,0:T(4,128)S(1)} %fusion.20, f32[512]{0:T(512)S(1)} %get-tuple-element.634, ...), channel_id=1, replica_groups=mesh['dp'=8,'seq'=32] {'seq'}, use_global_device_ids=true, to_apply=%region_19.20 | all-reduce | flops 2566 | bytes 20528 | tf_op jit(solution)/shard_map/psum | solution.py:17
  977.3 25.2 %all-reduce.1 = (f32[]{:T(128)}, f32[4,512]{1,0:T(4,128)S(1)}, f32[512]{0:T(512)S(1)}, f32[4]{0:T(128)}) all-reduce(f32[]{:T(128)} %get-tuple-element.617, f32[4,512]{1,0:T(4,128)S(1)} %get-tuple-element.619, f32[512]{0:T(512)S(1)} %get-tuple-element.620, f32[4]{0:T(128)S(1)} %get-tuple-element.621), channel_id=1, replica_groups=mesh['dp'=8,'seq'=32] {'dp'}, use_global_device_ids=true, to_apply=%region_20.21 | all-reduce | flops 2565 | bytes 20520 | tf_op jit(solution)/shard_map/psum | solution.py:17
  (1138 shorter events, 298.7 us)
Async XLA Ops:
  7.2 659.3 %copy-start = (bf16[4,512]{1,0:T(4,128)(2,1)S(1)}, bf16[4,512]{1,0:T(4,128)(2,1)}, u32[]{:S(2)}) copy-start(bf16[4,512]{1,0:T(4,128)(2,1)} %param.22) | copy-start | bytes 12292
  7.2 3.1 copy-start.4
  7.2 67.9 %all-gather.6.cloned.1.call-start = ((), (), s32[]{:S(2)}) async-start(), calls=%async_computation.4 | async-start | bytes 4325376 | tf_op jit(solution)/shard_map/all_gather | solution.py:113
  7.9 657.6 %reduce-scatter.4.cloned.1.call-start = ((), (), s32[]{:S(2)}) async-start(), calls=%async_computation.5 | async-start | bytes 2162688
  494.1 2.1 copy-start.1
  494.1 2.1 copy-start.2
  496.1 170.4 %copy-start.5 = (f32[4]{0:T(128)S(1)}, f32[4]{0:T(128)}, u32[]{:S(2)}) copy-start(f32[4]{0:T(128)} %param.23) | copy-start | bytes 52
  496.1 261.2 %all-gather.4.cloned.1.call-start = ((), (), s32[]{:S(2)}) async-start(), calls=%async_computation.2 | async-start | bytes 4325376 | tf_op jit(solution)/shard_map/all_gather | solution.py:145
  666.4 68.1 %copy-start.3 = (f32[4,128]{1,0:T(4,128)}, f32[4,128]{1,0:T(4,128)S(1)}, u32[]{:S(2)}) copy-start(f32[4,128]{1,0:T(4,128)S(1)} %copy.52) | copy-start | bytes 6148
  668.2 166.8 %all-reduce.4.cloned.1.call-start = ((), (), s32[]{:S(2)}) async-start(), calls=%async_computation.3 | async-start | bytes 1048576 | tf_op jit(solution)/shard_map/psum | solution.py:152
Sparse Core Ops, SparseCore 0:
  10.6 64.5 all-gather.5
  496.2 169.2 reduce-scatter.3
  668.7 88.6 all-gather.3
  762.4 72.5 all-reduce.3
